TPU v7x, 32 devices: a whole 2x2x4 slice. The times are simulated.
32 devices in a mesh: seq: 2 (over y), dom: 8 (over z, x), tm: 2 (over core).
Axes of the slice: x: 2, y: 2, z: 4, core: 2. Of those that a mesh axis runs over, the one named last changes fastest.
Arguments:
- particles: bfloat16 [4, 1536, 128], P('tm', ('seq', 'dom')), parts along dimension 1, may hold values from -6 to 6
- log_weight: float32 [4, 1536], P('tm', ('seq', 'dom')), parts along dimension 1, may hold values from -13 to 313
- trans_weight: bfloat16 [128, 128], replicated, may hold values from -0.5 to 0.5
- precision: float32 [128], replicated, may hold values from 0.2 to 2
Outputs:
- smoothed: float32 [4, 1536], P('tm', ('seq', 'dom')), parts along dimension 1
- score: float32 [256, 128], P('seq'), parts along dimension 0
There are 2 independent parts, one for each index of `seq`. A program takes and returns all parts, laid end to end along the dimension named above; an argument that names none is the same for every part. Nothing has to cross between parts.
All inputs are finite; a program needn't handle non-finite values.
Results may differ from a plain program's by a relative error of at most 0.0061.
Values may be sent and summed in bfloat16 or wider, within the bound.
A program may use at most 64 MiB of HBM per device.

v0:
```python
import jax
import jax.numpy as jnp
from jax import lax
from jax.sharding import PartitionSpec as P

exact_mode = lax.Precision.HIGHEST


def from_behind(x, axis, by):
    size = lax.axis_size(axis)
    pairs = [(i, i + by) for i in range(size) if 0 <= i + by < size]
    return lax.ppermute(x, axis, pairs)


def block_size(length):
    best = 1
    for trial in range(1, min(length, 512) + 1):
        if length % trial == 0:
            best = trial
    return best


def project_rows(rows, precision, weight_full):
    return jnp.dot(rows.astype(jnp.float32) * precision, weight_full, precision=exact_mode).astype(
        jnp.bfloat16
    )


def pair_scores(row_proj, column_rows, column_bias):
    return (
        jnp.einsum("id,jd->ij", row_proj, column_rows, preferred_element_type=jnp.float32)
        + column_bias[None, :]
    )


def make_norm_fold(row_proj, bias_row, carried, block_in, first_row):
    length = block_in.shape[0]
    size = block_size(length)

    def inner(position, state):
        row_top, row_total = state
        offset = position * size
        column_rows = lax.dynamic_slice_in_dim(block_in, offset, size, 0)
        bias_part = lax.dynamic_slice_in_dim(bias_row, first_row + offset, size, 0)
        scores = pair_scores(row_proj, column_rows, bias_part)
        new_top = jnp.maximum(row_top, jnp.max(scores, axis=1))
        row_total = row_total * jnp.exp(row_top - new_top) + jnp.sum(
            jnp.exp(scores - new_top[:, None]), axis=1
        )
        return (new_top, row_total)

    return lax.fori_loop(0, length // size, inner, carried)


def make_column_fold(row_proj, bias_row, row_norm, row_weight, carried, block_in, first_row):
    length = block_in.shape[0]
    size = block_size(length)

    def inner(position, state):
        moved, column_sums = state
        offset = position * size
        column_rows = lax.dynamic_slice_in_dim(block_in, offset, size, 0)
        bias_part = lax.dynamic_slice_in_dim(bias_row, first_row + offset, size, 0)
        scores = pair_scores(row_proj, column_rows, bias_part)
        backward = (row_weight[:, None] * jnp.exp(scores - row_norm[:, None])).astype(jnp.bfloat16)
        moved = moved + jnp.dot(backward, column_rows, preferred_element_type=jnp.float32)
        column_sums = lax.dynamic_update_slice_in_dim(
            column_sums, jnp.sum(backward.astype(jnp.float32), axis=0), first_row + offset, 0
        )
        return (moved, column_sums)

    return lax.fori_loop(0, length // size, inner, carried)


def shards(particles, log_weight, trans_weight, precision):
    steps_here, rows_here, width = particles.shape
    tm_count = lax.axis_size("tm")
    dom_count = lax.axis_size("dom")
    total_rows = rows_here * dom_count
    tm_place = lax.axis_index("tm")
    is_last = tm_place == tm_count - 1
    weight_full = trans_weight.astype(jnp.float32)
    boundary = from_behind(particles[0], "tm", -1)
    later_sets = [particles[1]] + [boundary]
    later_proj = [project_rows(rows, precision, weight_full) for rows in later_sets]
    biases = []
    for k in range(steps_here):
        predicted = jnp.dot(particles[k], trans_weight.T, preferred_element_type=jnp.float32)
        biases.append(log_weight[k] - 0.5 * jnp.sum(precision * predicted * predicted, axis=1))
    local_bias = jnp.stack(biases)
    full_bias = lax.all_gather(local_bias, "dom", axis=1, tiled=True)
    row_norms = []
    whole = lax.all_gather(particles, "dom", axis=1, tiled=True)
    for k in range(steps_here):
        start_state = (
            jnp.full((rows_here,), -jnp.inf, jnp.float32),
            jnp.zeros((rows_here,), jnp.float32),
        )
        row_top, row_total = make_norm_fold(later_proj[k], full_bias[k], start_state, whole[k], 0)
        row_norms.append(row_top + jnp.log(row_total))
    final_logs = log_weight[steps_here - 1]
    global_top = lax.pmax(jnp.max(final_logs), "dom")
    global_total = lax.psum(jnp.sum(jnp.exp(final_logs - global_top)), "dom")
    final_weights = jnp.exp(final_logs - global_top) / global_total
    carried = (
        jnp.zeros((steps_here, rows_here), jnp.float32),
        jnp.zeros((width, width), jnp.float32),
    )
    for r in range(tm_count):
        if r == 0:
            incoming = jnp.zeros((rows_here,), jnp.float32)
        else:
            incoming = from_behind(carried[0][0], "tm", -1)
        owner = tm_count - 1 - r
        backward_partial_value = jnp.zeros((width, width), jnp.float32)
        outputs = [None] * steps_here
        row_weight = incoming
        for backward_k in range(steps_here - 1, -1, -1):
            column_rows = particles[backward_k]
            backward_start_state = (
                jnp.zeros((rows_here, width), jnp.float32),
                jnp.zeros((total_rows,), jnp.float32),
            )
            moved, column_sums = make_column_fold(
                later_proj[backward_k],
                full_bias[backward_k],
                row_norms[backward_k],
                row_weight,
                backward_start_state,
                whole[backward_k],
                0,
            )
            column_weights = lax.psum_scatter(column_sums, "dom", scatter_dimension=0, tiled=True)
            outer = jnp.dot(
                later_sets[backward_k].astype(jnp.float32).T, moved, precision=exact_mode
            )
            column_float = column_rows.astype(jnp.float32)
            moment = jnp.dot(
                column_float.T * column_weights[None, :], column_float, precision=exact_mode
            )
            backward_partial_value = backward_partial_value + precision[:, None] * (
                outer - jnp.dot(weight_full, moment, precision=exact_mode)
            )
            if backward_k == steps_here - 1:
                column_weights = jnp.where(is_last, final_weights, column_weights)
            outputs[backward_k] = column_weights
            row_weight = column_weights
        is_owner = tm_place == owner
        carried = (
            jnp.where(is_owner, jnp.stack(outputs), carried[0]),
            jnp.where(is_owner, backward_partial_value, carried[1]),
        )
    stacked, partial_value = carried
    score = lax.psum(partial_value, ("dom", "tm"))
    return (stacked * total_rows, score)


def solution(mesh):
    placed = (P("tm", ("seq", "dom"), None), P("tm", ("seq", "dom")), P(), P())
    return jax.shard_map(
        shards,
        mesh=mesh,
        in_specs=placed,
        out_specs=(P("tm", ("seq", "dom")), P("seq", None)),
        check_vma=False,
    )
```

profile of v0, /device:TPU:1, one launch (start us, length us, event | category | flops | bytes accessed | tf_op | source)
XLA Modules:
  0.0 266.2 jit_solution(9784451875654501515)
XLA Ops:
  7.2 0.8 slice_bitcast_fusion.2
  8.0 2.1 collective-permute-start
  10.1 27.3 %all_gather.6 = bf16[2,768,128]{2,1,0:T(8,128)(2,1)S(1)} all-gather(bf16[2,96,128]{2,1,0:T(8,128)(2,1)S(1)} %copy-done.1), channel_id=1, replica_groups=mesh['seq'=2,'dom'=8,'tm'=2] {'dom'}, dimensions={1}, use_global_device_ids=true | all-gather | bytes 442368 | tf_op jit(solution)/shard_map/all_gather | solution.py:93
  38.1 0.6 copy-done.3
  38.8 0.6 slice_reduce_fusion.2
  39.4 17.9 %pmax.7 = f32[]{:T(128)} all-reduce(f32[]{:T(128)} %slice_reduce_fusion.2), channel_id=1, replica_groups=mesh['seq'=2,'dom'=8,'tm'=2] {'dom'}, use_global_device_ids=true, to_apply=%region_3.4 | all-reduce | flops 1 | bytes 8 | tf_op jit(solution)/shard_map/pmax | solution.py:102
  57.3 1.2 fusion.81
  58.5 13.1 %all-gather = f32[8,96,2]{1,2,0:T(2,128)S(1)} all-gather(f32[1,96,2]{1,2,0:T(2,128)S(1)} %maximum_bitcast_fusion), channel_id=1, replica_groups=mesh['seq'=2,'dom'=8,'tm'=2] {'dom'}, dimensions={0}, use_global_device_ids=true | all-gather | bytes 6912 | tf_op jit(solution)/shard_map/all_gather | solution.py:91
  71.7 1.2 while.98
  73.0 0.6 copy-done.4
  75.0 1.2 while.96
  76.3 1.5 while.97
  77.7 16.1 %all-reduce.4 = (f32[768]{0:T(1024)S(1)}, f32[]{:T(128)}) all-reduce(f32[768]{0:T(1024)S(1)} %get-tuple-element.769, f32[]{:T(128)} %get-tuple-element.1041), channel_id=2, replica_groups=mesh['seq'=2,'dom'=8,'tm'=2] {'dom'}, use_global_device_ids=true, to_apply=%region_13.0.clone | all-reduce | flops 769 | bytes 6152
  93.8 1.3 broadcast_select_fusion.5
  95.1 1.5 while.99
  96.6 13.6 %all-reduce.1 = f32[768]{0:T(1024)S(1)} all-reduce(f32[768]{0:T(1024)S(1)} %get-tuple-element.772), channel_id=3, replica_groups=mesh['seq'=2,'dom'=8,'tm'=2] {'dom'}, use_global_device_ids=true, to_apply=%region_21.22.clone | all-reduce | flops 768 | bytes 6144
  110.4 21.5 %collective-permute-start.1 = (f32[96]{0:T(128)S(1)}, f32[96]{0:T(128)S(1)}, u32[]{:S(2)}, u32[]{:S(2)}) collective-permute-start(f32[96]{0:T(128)S(1)} %slice_bitcast_fusion.3), channel_id=1, source_target_pairs={{1,0},{3,2},{5,4},{7,6},{9,8},{11,10},{13,12},{15,14},{17,16},{19,... | collective-permute-start | bytes 1160 | tf_op jit(solution)/shard_map/ppermute | solution.py:12
  133.6 1.5 while.100
  135.0 15.5 %all-reduce.2 = f32[768]{0:T(1024)S(1)} all-reduce(f32[768]{0:T(1024)S(1)} %get-tuple-element.773), channel_id=4, replica_groups=mesh['seq'=2,'dom'=8,'tm'=2] {'dom'}, use_global_device_ids=true, to_apply=%region_25.26.clone | all-reduce | flops 768 | bytes 6144
  150.6 1.5 while.101
  152.1 13.6 %all-reduce.3 = f32[768]{0:T(1024)S(1)} all-reduce(f32[768]{0:T(1024)S(1)} %get-tuple-element.774), channel_id=5, replica_groups=mesh['seq'=2,'dom'=8,'tm'=2] {'dom'}, use_global_device_ids=true, to_apply=%region_29.30.clone | all-reduce | flops 768 | bytes 6144
  167.3 0.9 fusion.48
  168.8 89.0 %all-reduce.7.cloned.1.call-done = f32[128,128]{0,1:T(8,128)} async-done(((f32[128,128]{0,1:T(8,128)}), f32[128,128]{0,1:T(8,128)}) %all-reduce.7.cloned.1.call-update) | async-done | bytes 65552 | tf_op jit(solution)/shard_map/psum | solution.py:154
  257.8 1.6 copy.10
  (110 shorter events, 13.6 us)
Async XLA Ops:
  7.2 30.2 %copy-start = (bf16[128,128]{1,0:T(8,128)(2,1)S(1)}, bf16[128,128]{1,0:T(8,128)(2,1)}, u32[]{:S(2)}) copy-start(bf16[128,128]{1,0:T(8,128)(2,1)} %param.18) | copy-start | bytes 98308
  7.2 2.9 %copy-start.1 = (bf16[2,96,128]{2,1,0:T(8,128)(2,1)S(1)}, bf16[2,96,128]{2,1,0:T(8,128)(2,1)}, u32[]{:S(2)}) copy-start(bf16[2,96,128]{2,1,0:T(8,128)(2,1)} %param.16) | copy-start | bytes 147460
  7.2 250.6 %all-reduce.7.cloned.1.call-start = ((), (), s32[]{:S(2)}) async-start(), calls=%async_computation | async-start | bytes 131072 | tf_op jit(solution)/shard_map/psum | solution.py:154
  8.0 29.4 %copy-start.2 = (f32[128]{0:T(128)S(1)}, f32[128]{0:T(128)}, u32[]{:S(2)}) copy-start(f32[128]{0:T(128)} %param.19) | copy-start | bytes 1540
  8.0 66.9 %collective-permute-start = (bf16[96,128]{1,0:T(8,128)(2,1)S(1)}, bf16[96,128]{1,0:T(8,128)(2,1)S(1)}, u32[]{:S(2)}, u32[]{:S(2)}) collective-permute-start(bf16[96,128]{1,0:T(8,128)(2,1)S(1)} %slice_bitcast_fusion.2), channel_id=1, source_target_pairs={{1,0},{3,2},{5,4},{7,6},{9,8},{11,10},{13,12},{15,14},{17,16},{19,... | collective-permute-start | bytes 73736 | tf_op jit(solution)/shard_map/ppermute | solution.py:12
  38.1 0.7 copy-start.3
  73.0 0.7 copy-start.4
  110.4 23.2 %collective-permute-start.1 = (f32[96]{0:T(128)S(1)}, f32[96]{0:T(128)S(1)}, u32[]{:S(2)}, u32[]{:S(2)}) collective-permute-start(f32[96]{0:T(128)S(1)} %slice_bitcast_fusion.3), channel_id=1, source_target_pairs={{1,0},{3,2},{5,4},{7,6},{9,8},{11,10},{13,12},{15,14},{17,16},{19,... | collective-permute-start | bytes 1160 | tf_op jit(solution)/shard_map/ppermute | solution.py:12
Sparse Core Ops, SparseCore 0:
  168.3 89.4 all-reduce.6
where the time goes:
time: 268 us; the launch traced here: 266 us
  blocking collectives  117 us (44%)
  waiting for transfers between devices  89 us (33%)
  starting transfers between devices  23.6 us (9%)
  between operations  14.9 us (6%)
  matrix products  8.92 us (3%)
  local copies, waits for them, and re-layouts  7.58 us (3%)
  other arithmetic  4.58 us (2%)
    psum x1, waiting for transfers between devices, shards(): score = lax.psum(partial_value, ('dom', 'tm'))  89 us
    unnamed x4, blocking collectives  58.9 us
    all_gather x1, blocking collectives, shards(): whole = lax.all_gather(particles, 'dom', axis=1, tiled=True)  27.3 us
    ppermute x2, starting transfers between devices, from_behind(): return lax.ppermute(x, axis, pairs)  23.6 us
    pmax x1, blocking collectives, shards(): global_top = lax.pmax(jnp.max(final_logs), 'dom')  17.9 us
    all_gather x1, blocking collectives, shards(): full_bias = lax.all_gather(local_bias, 'dom', axis=1, tiled=True)  13.1 us
  transfers between devices with their start and end apart: 3, of which 1 were waited for; matrix products, arithmetic and copies ran while one was open for 2% of the time, Pallas kernels for 0%

commit v1 on v0

--- a/solution.py
+++ b/solution.py
@@ -1,6 +1,10 @@
+import functools
+
 import jax
 import jax.numpy as jnp
 from jax import lax
+from jax.experimental import pallas as pl
+from jax.experimental.pallas import tpu as pltpu
 from jax.sharding import PartitionSpec as P
 
 exact_mode = lax.Precision.HIGHEST
@@ -155,10 +159,229 @@
     return (stacked * total_rows, score)
 
 
+MESH = pl.DeviceIdType.MESH
+EXTRA = 16
+MOST_ROWS = 1024
+
+
+def nt_dot(a, b):
+    return lax.dot_general(a, b, (((1,), (1,)), ((), ())), preferred_element_type=jnp.float32)
+
+
+def tn_dot(a, b):
+    return lax.dot_general(a, b, (((0,), (0,)), ((), ())), preferred_element_type=jnp.float32)
+
+
+def nn_dot(a, b):
+    return jnp.dot(a, b, preferred_element_type=jnp.float32)
+
+
+def split_three(x):
+    high = x.astype(jnp.bfloat16)
+    rest = x - high.astype(jnp.float32)
+    middle = rest.astype(jnp.bfloat16)
+    low = (rest - middle.astype(jnp.float32)).astype(jnp.bfloat16)
+    return high, middle, low
+
+
+def smoother_kernel(
+    n_dom, x_ref, lw_ref, w_ref, p_ref, smoothed_ref, score_ref,
+    held, kernel_rows, inverse_norm, bias, weights, stage, send_sem, recv_sem,
+):
+    rows, width = x_ref.shape[1:]
+    total = n_dom * rows
+    steps = 4
+    half = total // 2
+    dom = lax.axis_index("dom")
+    tm = lax.axis_index("tm")
+    group, side = dom // 2, dom % 2
+    groups = n_dom // 2
+    across = dom + 1 - 2 * side
+    other = 1 - tm
+    mine = tm * n_dom + dom
+    peers = [lax.rem(group + k, groups) * 2 + side for k in range(1, groups)]
+
+    barrier = pltpu.get_barrier_semaphore()
+    targets = [(peer, tm) for peer in peers] + [(across, tm), (dom, other)]
+    for to_dom, to_tm in targets:
+        pl.semaphore_signal(
+            barrier, inc=1, device_id={"dom": to_dom, "tm": to_tm}, device_id_type=MESH
+        )
+
+    weight = w_ref[...]
+    p_row = p_ref[...]
+    p_down = jnp.broadcast_to(p_row, (width, width)).T
+    stage[...] = jnp.zeros_like(stage)
+    terms = []
+    for k in range(2):
+        x_k = x_ref[k]
+        held[mine, k * rows : (k + 1) * rows, :] = x_k
+        predicted = nt_dot(weight, x_k)
+        energy = jnp.sum(p_down[:, :rows] * predicted * predicted, axis=0, keepdims=True)
+        terms.append(lw_ref[k : k + 1, :] - 0.5 * energy)
+    terms.append(lw_ref[1:2, :])
+    for q in range(3):
+        for piece, value in enumerate(split_three(terms[q])):
+            row = 3 * piece + q
+            stage[row : row + 1, 0:rows] = value.astype(jnp.float32)
+    held[mine, 2 * rows : 2 * rows + EXTRA, :] = stage[...].astype(jnp.bfloat16)
+
+    pl.semaphore_wait(barrier, len(targets))
+
+    sends = []
+
+    def send(slot, to_dom, to_tm):
+        copy = pltpu.make_async_remote_copy(
+            src_ref=held.at[slot],
+            dst_ref=held.at[slot],
+            send_sem=send_sem.at[len(sends)],
+            recv_sem=recv_sem.at[slot],
+            device_id={"dom": to_dom, "tm": to_tm},
+            device_id_type=MESH,
+        )
+        copy.start()
+        sends.append(copy)
+
+    def arrive(slot):
+        pltpu.make_async_remote_copy(
+            src_ref=held.at[slot],
+            dst_ref=held.at[slot],
+            send_sem=send_sem.at[0],
+            recv_sem=recv_sem.at[slot],
+            device_id={"dom": dom, "tm": other},
+            device_id_type=MESH,
+        ).wait_recv()
+
+    for peer in peers:
+        send(mine, peer, tm)
+    send(mine, across, tm)
+    send(mine, dom, other)
+
+    scaled = jnp.concatenate(
+        split_three(p_down * weight.astype(jnp.float32)), axis=1
+    )
+
+    for peer in peers:
+        slot = tm * n_dom + peer
+        arrive(slot)
+        send(slot, across, tm)
+        send(slot, dom, other)
+    for pair in [across] + [peer + 1 - 2 * side for peer in peers]:
+        slot = tm * n_dom + pair
+        arrive(slot)
+        send(slot, dom, other)
+    for d in range(n_dom):
+        arrive(other * n_dom + d)
+
+    def set_of(t, first=0, count=n_dom):
+        at = (t // 2) * n_dom + first
+        k = t % 2
+        return held[at : at + count, k * rows : (k + 1) * rows, :].reshape(count * rows, width)
+
+    line = lax.broadcasted_iota(jnp.int32, (EXTRA, 3 * width), 0)
+    which = lax.broadcasted_iota(jnp.int32, (EXTRA, 3 * width), 1) // width
+    pick = jnp.where((line < 9) & (line % 3 == which), 1.0, 0.0).astype(jnp.bfloat16)
+    for s in range(2 * n_dom):
+        spread = tn_dot(held[s, 2 * rows : 2 * rows + EXTRA, :], pick)
+        at = (s % n_dom) * rows
+        for k in range(2):
+            t = 2 * (s // n_dom) + k
+            part = spread[:rows, k * width : (k + 1) * width]
+            if t == steps - 1:
+                part = spread[:rows, 2 * width :]
+            bias[t, at : at + rows, :] = part
+
+    last = bias[steps - 1]
+    last = jnp.exp(last - jnp.max(last, axis=0, keepdims=True))
+    weights[steps - 1] = last / jnp.sum(last, axis=0, keepdims=True)
+
+    for t in range(steps - 2, -1, -1):
+        for h in range(2):
+            later = set_of(t + 1, h * (n_dom // 2), n_dom // 2)
+            wide = nn_dot(later, scaled)
+            projected = (
+                wide[:, :width] + (wide[:, width : 2 * width] + wide[:, 2 * width :])
+            ).astype(jnp.bfloat16)
+            scores = nt_dot(set_of(t), projected)
+            scores = scores + jnp.concatenate([bias[t]] * (half // width), axis=1)
+            top = jnp.max(scores, axis=0, keepdims=True)
+            terms = jnp.exp(scores - top)
+            inverse = 1.0 / jnp.sum(terms, axis=0, keepdims=True)
+            kernel_rows[t, :, h * half : (h + 1) * half] = terms.astype(jnp.bfloat16)
+            for b in range(half // width):
+                at = h * half + b * width
+                inverse_norm[t, at : at + width, :] = jnp.broadcast_to(
+                    inverse[:, b * width : (b + 1) * width], (width, width)
+                ).T
+
+    score = jnp.zeros((width, width), jnp.float32)
+    for t in range(steps - 2, -1, -1):
+        ratio = weights[t + 1] * inverse_norm[t]
+        right = jnp.concatenate(
+            [(ratio * set_of(t + 1).astype(jnp.float32)).astype(jnp.bfloat16), ratio.astype(jnp.bfloat16)],
+            axis=1,
+        )
+        both = nn_dot(kernel_rows[t], right)
+        now = both[:, width:]
+        weights[t] = now
+        columns = set_of(t)
+        predicted = nt_dot(columns, weight)
+        residual = (both[:, :width] - predicted * now) * p_row
+        score = score + tn_dot(residual.astype(jnp.bfloat16), columns)
+    score_ref[...] = score
+    first = pl.multiple_of(dom * rows, rows)
+    for k in range(2):
+        own = weights[2 * tm + k, pl.ds(first, rows), :] * total
+        smoothed_ref[k : k + 1, :] = own.T[0:1, :]
+    for copy in sends:
+        copy.wait_send()
+
+
+def fused(particles, log_weight, trans_weight, precision):
+    steps_here, rows, width = particles.shape
+    n_dom = lax.axis_size("dom")
+    total = n_dom * rows
+    whole = pl.BlockSpec(memory_space=pltpu.VMEM)
+    copies = (n_dom // 2 - 1) * 3 + 2 + n_dom // 2
+    return pl.pallas_call(
+        functools.partial(smoother_kernel, n_dom),
+        out_shape=(
+            jax.ShapeDtypeStruct((steps_here, rows), jnp.float32),
+            jax.ShapeDtypeStruct((width, width), jnp.float32),
+        ),
+        in_specs=[whole] * 4,
+        out_specs=(whole, whole),
+        scratch_shapes=[
+            pltpu.VMEM((2 * n_dom, 2 * rows + EXTRA, width), jnp.bfloat16),
+            pltpu.VMEM((3, total, total), jnp.bfloat16),
+            pltpu.VMEM((3, total, width), jnp.float32),
+            pltpu.VMEM((4, total, width), jnp.float32),
+            pltpu.VMEM((4, total, width), jnp.float32),
+            pltpu.VMEM((EXTRA, width), jnp.float32),
+            pltpu.SemaphoreType.DMA((copies,)),
+            pltpu.SemaphoreType.DMA((2 * n_dom,)),
+        ],
+        compiler_params=pltpu.CompilerParams(
+            collective_id=0, has_side_effects=True, vmem_limit_bytes=48 * 2**20
+        ),
+    )(particles, log_weight, trans_weight, precision.reshape(1, width))
+
+
+def plan(particles, log_weight, trans_weight, precision):
+    steps_here, rows, width = particles.shape
+    n_dom = lax.axis_size("dom")
+    total = n_dom * rows
+    small = total <= MOST_ROWS and total % (2 * width) == 0 and rows <= width and rows % 16 == 0
+    shaped = n_dom % 2 == 0 and lax.axis_size("tm") == 2 and steps_here == 2 and width == 128
+    if small and shaped:
+        return fused(particles, log_weight, trans_weight, precision)
+    return shards(particles, log_weight, trans_weight, precision)
+
+
 def solution(mesh):
     placed = (P("tm", ("seq", "dom"), None), P("tm", ("seq", "dom")), P(), P())
     return jax.shard_map(
-        shards,
+        plan,
         mesh=mesh,
         in_specs=placed,
         out_specs=(P("tm", ("seq", "dom")), P("seq", None)),

time: 268 us -> 26.3 us (0.10)
  blocking collectives: 117 us -> 0 us
  waiting for transfers between devices: 89 us -> 0 us
  starting transfers between devices: 23.6 us -> 0 us
  Pallas kernels: 0 us -> 22 us
  between operations: 14.9 us -> 0.66 us
  matrix products: 8.92 us -> 0 us
  other arithmetic: 4.58 us -> 0 us
  local copies, waits for them, and re-layouts: 7.58 us -> 3.43 us
    psum x1 -> x0, waiting for transfers between devices: 89 us -> none  [shards(): score = lax.psum(partial_value, ('dom', 'tm'))]
    unnamed x4 -> x0, blocking collectives: 58.9 us -> none
    all_gather x2 -> x0, blocking collectives: 40.4 us -> none  [the longest x1 27.3 us: shards(): whole = lax.all_gather(particles, 'dom', axis=1, tiled=True)]
    ppermute x2 -> x0, starting transfers between devices: 23.6 us -> none  [from_behind(): return lax.ppermute(x, axis, pairs)]
    pallas_call x0 -> x1, Pallas kernels: none -> 22 us  [fused(): pl.pallas_call(functools.partial(smoother_kernel, n_dom), out_shape=(jax....]
    pmax x1 -> x0, blocking collectives: 17.9 us -> none  [shards(): global_top = lax.pmax(jnp.max(final_logs), 'dom')]
    dot_general x36 -> x0, matrix products: 8.92 us -> none  [the longest x12 2.76 us: pair_scores(): jnp.einsum('id,jd->ij', row_proj, column_rows, preferred_element_type=jnp...]
  transfers between devices with their start and end apart: 3 -> 0, of which waited for: 1 -> 0; matrix products, arithmetic and copies ran while one was open for 2% -> 0% of each run, Pallas kernels for 0% -> 0%
where the time goes in v1:
time: 26.3 us; the launch traced here: 26.1 us
  Pallas kernels  22 us (84%)
  local copies, waits for them, and re-layouts  3.43 us (13%)
  between operations  0.66 us (3%)
    pallas_call x1, Pallas kernels, fused(): pl.pallas_call(functools.partial(smoother_kernel, n_dom), out_shape=(jax....  22 us
    unnamed x10, local copies, waits for them, and re-layouts  3.43 us

profile of v1, /device:TPU:1, one launch (start us, length us, event | category | flops | bytes accessed | tf_op | source)
XLA Modules:
  0.0 26.1 jit_solution(8433390837336847588)
XLA Ops:
  0.6 0.0 copy-start.3
  0.6 0.0 copy-start.2
  0.7 0.6 %copy-done.3 = f32[128]{0:T(128)S(1)} copy-done((f32[128]{0:T(128)S(1)}, f32[128]{0:T(128)}, u32[]{:S(2)}) %copy-start.3) | copy-done | bytes 536
  1.3 0.0 copy-done.2
  1.3 0.0 copy-start
  1.3 0.8 %copy-done = bf16[2,96,128]{2,1,0:T(8,128)(2,1)S(1)} copy-done((bf16[2,96,128]{2,1,0:T(8,128)(2,1)S(1)}, bf16[2,96,128]{2,1,0:T(8,128)(2,1)}, u32[]{:S(2)}) %copy-start) | copy-done | bytes 49176
  2.1 0.0 copy-start.1
  2.1 0.8 %copy-done.1 = bf16[128,128]{1,0:T(8,128)(2,1)S(1)} copy-done((bf16[128,128]{1,0:T(8,128)(2,1)S(1)}, bf16[128,128]{1,0:T(8,128)(2,1)}, u32[]{:S(2)}) %copy-start.1) | copy-done | bytes 32792
  2.9 22.0 %shard_map.59 = (f32[2,96]{1,0:T(2,128)S(1)}, f32[128,128]{1,0:T(8,128)S(1)}) custom-call(bf16[2,96,128]{2,1,0:T(8,128)(2,1)S(1)} %copy-done, f32[2,96]{1,0:T(2,128)S(1)} %copy-done.2, bf16[128,128]{1,0:T(8,128)(2,1)S(1)} %copy-done.1, f32[1,128]{1,0:T(1,128)S(1)} %bitcast.1), custom_call_target="tpu_custom_call" | custom-call | tf_op jit(solution)/shard_map/pallas_call | solution.py:346
  24.9 0.6 %copy.8 = f32[2,96]{1,0:T(2,128)} copy(f32[2,96]{1,0:T(2,128)S(1)} %get-tuple-element.4) | data formatting | bytes 1536
  25.5 0.6 %copy.9 = f32[128,128]{1,0:T(8,128)} copy(f32[128,128]{1,0:T(8,128)S(1)} %get-tuple-element.5) | data formatting | bytes 131072
Async XLA Ops:
  0.6 0.7 %copy-start.3 = (f32[128]{0:T(128)S(1)}, f32[128]{0:T(128)}, u32[]{:S(2)}) copy-start(f32[128]{0:T(128)} %param.7) | copy-start | bytes 1540
  0.6 0.7 %copy-start.2 = (f32[2,96]{1,0:T(2,128)S(1)}, f32[2,96]{1,0:T(2,128)}, u32[]{:S(2)}) copy-start(f32[2,96]{1,0:T(2,128)} %lw_ref.1) | copy-start | bytes 2308
  1.3 0.8 %copy-start = (bf16[2,96,128]{2,1,0:T(8,128)(2,1)S(1)}, bf16[2,96,128]{2,1,0:T(8,128)(2,1)}, u32[]{:S(2)}) copy-start(bf16[2,96,128]{2,1,0:T(8,128)(2,1)} %x_ref.1) | copy-start | bytes 147460
  2.1 0.8 %copy-start.1 = (bf16[128,128]{1,0:T(8,128)(2,1)S(1)}, bf16[128,128]{1,0:T(8,128)(2,1)}, u32[]{:S(2)}) copy-start(bf16[128,128]{1,0:T(8,128)(2,1)} %w_ref.1) | copy-start | bytes 98308

commit v2 on v1

--- a/solution.py
+++ b/solution.py
@@ -185,21 +185,39 @@
 
 
 def smoother_kernel(
-    n_dom, x_ref, lw_ref, w_ref, p_ref, smoothed_ref, score_ref,
-    held, kernel_rows, inverse_norm, bias, weights, stage, send_sem, recv_sem,
+    n_dom, x_hbm, lw_hbm, w_hbm, p_hbm, smoothed_ref, score_ref,
+    lw_ref, w_ref, p_ref, held, kernel_rows, stats, inverse_norm, bias, weights, stage, in_sem, send_sem, recv_sem,
 ):
-    rows, width = x_ref.shape[1:]
+    rows, width = x_hbm.shape[1:]
     total = n_dom * rows
     steps = 4
     half = total // 2
     dom = lax.axis_index("dom")
     tm = lax.axis_index("tm")
     group, side = dom // 2, dom % 2
-    groups = n_dom // 2
+    high, low = group // 2, group % 2
+    near = 2 * high + 1 - low
+    mirror = 2 * (1 - high) + low
+    opposite = 2 * (1 - high) + 1 - low
     across = dom + 1 - 2 * side
     other = 1 - tm
-    mine = tm * n_dom + dom
-    peers = [lax.rem(group + k, groups) * 2 + side for k in range(1, groups)]
+    mine = tm * n_dom + group
+    peers = [2 * g + side for g in (near, mirror, opposite)]
+
+    loads = [
+        pltpu.make_async_copy(source, target, in_sem.at[i])
+        for i, (source, target) in enumerate(
+            [
+                (w_hbm, w_ref),
+                (p_hbm, p_ref),
+                (lw_hbm, lw_ref),
+                (x_hbm.at[0], held.at[mine, 0:rows]),
+                (x_hbm.at[1], held.at[mine, rows : 2 * rows]),
+            ]
+        )
+    ]
+    for load in loads:
+        load.start()
 
     barrier = pltpu.get_barrier_semaphore()
     targets = [(peer, tm) for peer in peers] + [(across, tm), (dom, other)]
@@ -208,14 +226,15 @@
             barrier, inc=1, device_id={"dom": to_dom, "tm": to_tm}, device_id_type=MESH
         )
 
+    for load in loads:
+        load.wait()
     weight = w_ref[...]
     p_row = p_ref[...]
     p_down = jnp.broadcast_to(p_row, (width, width)).T
     stage[...] = jnp.zeros_like(stage)
     terms = []
     for k in range(2):
-        x_k = x_ref[k]
-        held[mine, k * rows : (k + 1) * rows, :] = x_k
+        x_k = held[mine, k * rows : (k + 1) * rows, :]
         predicted = nt_dot(weight, x_k)
         energy = jnp.sum(p_down[:, :rows] * predicted * predicted, axis=0, keepdims=True)
         terms.append(lw_ref[k : k + 1, :] - 0.5 * energy)
@@ -230,108 +249,128 @@
 
     sends = []
 
-    def send(slot, to_dom, to_tm):
-        copy = pltpu.make_async_remote_copy(
-            src_ref=held.at[slot],
-            dst_ref=held.at[slot],
-            send_sem=send_sem.at[len(sends)],
-            recv_sem=recv_sem.at[slot],
+    def transfer(source, target, index, to_dom, to_tm):
+        return pltpu.make_async_remote_copy(
+            src_ref=held.at[source],
+            dst_ref=held.at[target],
+            send_sem=send_sem.at[index],
+            recv_sem=recv_sem.at[target],
             device_id={"dom": to_dom, "tm": to_tm},
             device_id_type=MESH,
         )
+
+    def send(source, target, to_dom, to_tm):
+        copy = transfer(source, target, len(sends), to_dom, to_tm)
         copy.start()
         sends.append(copy)
 
     def arrive(slot):
-        pltpu.make_async_remote_copy(
-            src_ref=held.at[slot],
-            dst_ref=held.at[slot],
-            send_sem=send_sem.at[0],
-            recv_sem=recv_sem.at[slot],
-            device_id={"dom": dom, "tm": other},
-            device_id_type=MESH,
-        ).wait_recv()
-
+        transfer(slot, slot, 0, dom, other).wait_recv()
+
+    base, far_base = tm * n_dom, other * n_dom
+    part = n_dom // 2
     for peer in peers:
-        send(mine, peer, tm)
-    send(mine, across, tm)
-    send(mine, dom, other)
-
-    scaled = jnp.concatenate(
-        split_three(p_down * weight.astype(jnp.float32)), axis=1
-    )
-
-    for peer in peers:
-        slot = tm * n_dom + peer
-        arrive(slot)
-        send(slot, across, tm)
-        send(slot, dom, other)
-    for pair in [across] + [peer + 1 - 2 * side for peer in peers]:
-        slot = tm * n_dom + pair
-        arrive(slot)
-        send(slot, dom, other)
-    for d in range(n_dom):
-        arrive(other * n_dom + d)
-
-    def set_of(t, first=0, count=n_dom):
-        at = (t // 2) * n_dom + first
-        k = t % 2
-        return held[at : at + count, k * rows : (k + 1) * rows, :].reshape(count * rows, width)
-
+        send(mine, mine, peer, tm)
+    send(mine, mine + part, across, tm)
+    send(mine, mine, dom, other)
+
+    scaled = jnp.concatenate(split_three(p_down * weight.astype(jnp.float32)), axis=1)
     line = lax.broadcasted_iota(jnp.int32, (EXTRA, 3 * width), 0)
     which = lax.broadcasted_iota(jnp.int32, (EXTRA, 3 * width), 1) // width
     pick = jnp.where((line < 9) & (line % 3 == which), 1.0, 0.0).astype(jnp.bfloat16)
-    for s in range(2 * n_dom):
-        spread = tn_dot(held[s, 2 * rows : 2 * rows + EXTRA, :], pick)
-        at = (s % n_dom) * rows
-        for k in range(2):
-            t = 2 * (s // n_dom) + k
-            part = spread[:rows, k * width : (k + 1) * width]
-            if t == steps - 1:
-                part = spread[:rows, 2 * width :]
-            bias[t, at : at + rows, :] = part
-
-    last = bias[steps - 1]
+
+    def set_of(at, k):
+        return held[pl.ds(at, part), k * rows : (k + 1) * rows, :].reshape(half, width)
+
+    def spread_bias(h):
+        for c in range(2):
+            for g in range(part):
+                s = c * n_dom + h * part + g
+                spread = tn_dot(held[s, 2 * rows : 2 * rows + EXTRA, :], pick)
+                for k in range(2):
+                    t = 2 * c + k
+                    q = 2 if t == steps - 1 else k
+                    bias[t, h, g * rows : (g + 1) * rows, :] = spread[:rows, q * width : (q + 1) * width]
+
+    def tile(t, column_at, column_k, row_at, row_k, j, i):
+        wide = nn_dot(set_of(row_at + i * part, row_k), scaled)
+        projected = (
+            wide[:, :width] + (wide[:, width : 2 * width] + wide[:, 2 * width :])
+        ).astype(jnp.bfloat16)
+        scores = nt_dot(set_of(column_at + j * part, column_k), projected)
+        scores = scores + jnp.concatenate([bias[t, j]] * (half // width), axis=1)
+        top = jnp.max(scores, axis=0, keepdims=True)
+        terms = jnp.exp(scores - top)
+        kernel_rows[t, j, :, i * half : (i + 1) * half] = terms.astype(jnp.bfloat16)
+        stats[t, 2 * j + i, 0:1, :] = top
+        stats[t, 2 * j + i, 1:2, :] = jnp.sum(terms, axis=0, keepdims=True)
+
+    own_t = (2 * tm, base, 0, base, 1)
+    middle_t = (1, 0, 1, n_dom, 0)
+    other_t = (2 * other, far_base, 0, far_base, 1)
+
+    for n, g in enumerate((near, mirror, opposite)):
+        arrive(base + g)
+        send(base + g, base + g + part, across, tm)
+        send(base + g, base + g, dom, other)
+        if n == 0:
+            arrive(base + part + group)
+            send(base + part + group, base + part + group, dom, other)
+    for g in range(part):
+        arrive(far_base + g)
+    spread_bias(0)
+    for case in (own_t, middle_t, other_t):
+        tile(*case, 0, 0)
+    for g in (near, mirror, opposite):
+        arrive(base + part + g)
+        send(base + part + g, base + part + g, dom, other)
+    for g in range(part):
+        arrive(far_base + part + g)
+    spread_bias(1)
+
+    last = bias[steps - 1].reshape(total, width)
     last = jnp.exp(last - jnp.max(last, axis=0, keepdims=True))
     weights[steps - 1] = last / jnp.sum(last, axis=0, keepdims=True)
 
-    for t in range(steps - 2, -1, -1):
-        for h in range(2):
-            later = set_of(t + 1, h * (n_dom // 2), n_dom // 2)
-            wide = nn_dot(later, scaled)
-            projected = (
-                wide[:, :width] + (wide[:, width : 2 * width] + wide[:, 2 * width :])
-            ).astype(jnp.bfloat16)
-            scores = nt_dot(set_of(t), projected)
-            scores = scores + jnp.concatenate([bias[t]] * (half // width), axis=1)
-            top = jnp.max(scores, axis=0, keepdims=True)
-            terms = jnp.exp(scores - top)
-            inverse = 1.0 / jnp.sum(terms, axis=0, keepdims=True)
-            kernel_rows[t, :, h * half : (h + 1) * half] = terms.astype(jnp.bfloat16)
-            for b in range(half // width):
-                at = h * half + b * width
-                inverse_norm[t, at : at + width, :] = jnp.broadcast_to(
-                    inverse[:, b * width : (b + 1) * width], (width, width)
-                ).T
+    for case in (own_t, middle_t, other_t):
+        for j, i in ((0, 1), (1, 0), (1, 1)):
+            tile(*case, j, i)
 
     score = jnp.zeros((width, width), jnp.float32)
     for t in range(steps - 2, -1, -1):
-        ratio = weights[t + 1] * inverse_norm[t]
-        right = jnp.concatenate(
-            [(ratio * set_of(t + 1).astype(jnp.float32)).astype(jnp.bfloat16), ratio.astype(jnp.bfloat16)],
-            axis=1,
-        )
-        both = nn_dot(kernel_rows[t], right)
-        now = both[:, width:]
-        weights[t] = now
-        columns = set_of(t)
-        predicted = nt_dot(columns, weight)
-        residual = (both[:, :width] - predicted * now) * p_row
-        score = score + tn_dot(residual.astype(jnp.bfloat16), columns)
+        for i in range(2):
+            tops = [stats[t, 2 * j + i, 0:1, :] for j in range(2)]
+            top = jnp.maximum(tops[0], tops[1])
+            scales = [jnp.exp(tops[j] - top) for j in range(2)]
+            norm = sum(scales[j] * stats[t, 2 * j + i, 1:2, :] for j in range(2))
+            for j in range(2):
+                inverse = scales[j] / norm
+                for b in range(half // width):
+                    at = i * half + b * width
+                    inverse_norm[t, j, at : at + width, :] = jnp.broadcast_to(
+                        inverse[:, b * width : (b + 1) * width], (width, width)
+                    ).T
+    for t in range(steps - 2, -1, -1):
+        at, k = (t // 2) * n_dom, t % 2
+        later_at, later_k = ((t + 1) // 2) * n_dom, (t + 1) % 2
+        later = jnp.concatenate([set_of(later_at + i * part, later_k) for i in range(2)], axis=0)
+        later = later.astype(jnp.float32)
+        for j in range(2):
+            ratio = weights[t + 1] * inverse_norm[t, j]
+            right = jnp.concatenate(
+                [(ratio * later).astype(jnp.bfloat16), ratio.astype(jnp.bfloat16)], axis=1
+            )
+            both = nn_dot(kernel_rows[t, j], right)
+            now = both[:, width:]
+            weights[t, j * half : (j + 1) * half, :] = now
+            columns = set_of(at + j * part, k)
+            predicted = nt_dot(columns, weight)
+            residual = (both[:, :width] - predicted * now).astype(jnp.bfloat16)
+            score = score + tn_dot(residual, columns)
     score_ref[...] = score
-    first = pl.multiple_of(dom * rows, rows)
+    first = pl.multiple_of(group * rows, rows)
     for k in range(2):
-        own = weights[2 * tm + k, pl.ds(first, rows), :] * total
+        own = weights[2 * tm + k, pl.ds(first, rows), :]
         smoothed_ref[k : k + 1, :] = own.T[0:1, :]
     for copy in sends:
         copy.wait_send()
@@ -343,28 +382,34 @@
     total = n_dom * rows
     whole = pl.BlockSpec(memory_space=pltpu.VMEM)
     copies = (n_dom // 2 - 1) * 3 + 2 + n_dom // 2
-    return pl.pallas_call(
+    smoothed, score = pl.pallas_call(
         functools.partial(smoother_kernel, n_dom),
         out_shape=(
             jax.ShapeDtypeStruct((steps_here, rows), jnp.float32),
             jax.ShapeDtypeStruct((width, width), jnp.float32),
         ),
-        in_specs=[whole] * 4,
+        in_specs=[pl.BlockSpec(memory_space=pltpu.HBM)] * 4,
         out_specs=(whole, whole),
         scratch_shapes=[
+            pltpu.VMEM((steps_here, rows), jnp.float32),
+            pltpu.VMEM((width, width), jnp.bfloat16),
+            pltpu.VMEM((1, width), jnp.float32),
             pltpu.VMEM((2 * n_dom, 2 * rows + EXTRA, width), jnp.bfloat16),
-            pltpu.VMEM((3, total, total), jnp.bfloat16),
-            pltpu.VMEM((3, total, width), jnp.float32),
-            pltpu.VMEM((4, total, width), jnp.float32),
+            pltpu.VMEM((3, 2, total // 2, total), jnp.bfloat16),
+            pltpu.VMEM((3, 4, 8, total // 2), jnp.float32),
+            pltpu.VMEM((3, 2, total, width), jnp.float32),
+            pltpu.VMEM((4, 2, total // 2, width), jnp.float32),
             pltpu.VMEM((4, total, width), jnp.float32),
             pltpu.VMEM((EXTRA, width), jnp.float32),
+            pltpu.SemaphoreType.DMA((5,)),
             pltpu.SemaphoreType.DMA((copies,)),
             pltpu.SemaphoreType.DMA((2 * n_dom,)),
         ],
         compiler_params=pltpu.CompilerParams(
-            collective_id=0, has_side_effects=True, vmem_limit_bytes=48 * 2**20
+            collective_id=0, has_side_effects=True, vmem_limit_bytes=64 * 2**20
         ),
     )(particles, log_weight, trans_weight, precision.reshape(1, width))
+    return smoothed * total, score * precision[:, None]
 
 
 def plan(particles, log_weight, trans_weight, precision):
@@ -372,7 +417,7 @@
     n_dom = lax.axis_size("dom")
     total = n_dom * rows
     small = total <= MOST_ROWS and total % (2 * width) == 0 and rows <= width and rows % 16 == 0
-    shaped = n_dom % 2 == 0 and lax.axis_size("tm") == 2 and steps_here == 2 and width == 128
+    shaped = n_dom == 8 and lax.axis_size("tm") == 2 and steps_here == 2 and width == 128
     if small and shaped:
         return fused(particles, log_weight, trans_weight, precision)
     return shards(particles, log_weight, trans_weight, precision)

time: 26.3 us -> 25.8 us (0.981)
  local copies, waits for them, and re-layouts: 3.43 us -> 0.77 us
  other arithmetic: 0 us -> 2.12 us
    unnamed x10 -> x4, local copies, waits for them, and re-layouts: 3.43 us -> 0.77 us
    mul x0 -> x2, other arithmetic: none -> 2.12 us  [fused(): return (smoothed * total, score * precision[:, None])]
where the time goes in v2:
time: 25.8 us; the launch traced here: 25.5 us
  Pallas kernels  22 us (85%)
  other arithmetic  2.12 us (8%)
  local copies, waits for them, and re-layouts  0.77 us (3%)
  between operations  0.65 us (3%)
    pallas_call x1, Pallas kernels, fused(): pl.pallas_call(functools.partial(smoother_kernel, n_dom), out_shape=(jax....  22 us
    mul x2, other arithmetic, fused(): return (smoothed * total, score * precision[:, None])  2.12 us
    unnamed x4, local copies, waits for them, and re-layouts  0.77 us

profile of v2, /device:TPU:1, one launch (start us, length us, event | category | flops | bytes accessed | tf_op | source)
XLA Modules:
  0.0 25.5 jit_solution(16268406310795969217)
XLA Ops:
  0.6 22.0 %shard_map.59 = (f32[2,96]{1,0:T(2,128)}, f32[128,128]{1,0:T(8,128)}) custom-call(bf16[2,96,128]{2,1,0:T(8,128)(2,1)} %x_hbm.1, f32[2,96]{1,0:T(2,128)} %lw_hbm.1, bf16[128,128]{1,0:T(8,128)(2,1)} %w_hbm.1, f32[1,128]{1,0:T(1,128)} %bitcast.1), custom_call_target="tpu_custom_call" | custom-call | tf_op jit(solution)/shard_map/pallas_call | solution.py:385
  22.6 0.0 copy-start.1
  22.7 0.7 %copy-done.1 = f32[2,96]{1,0:T(2,128)S(1)} copy-done((f32[2,96]{1,0:T(2,128)S(1)}, f32[2,96]{1,0:T(2,128)}, u32[]{:S(2)}) %copy-start.1) | copy-done | bytes 792
  23.3 0.0 copy-start
  23.3 0.6 %broadcast_multiply_fusion.1 = f32[2,96]{1,0:T(2,128)} fusion(f32[2,96]{1,0:T(2,128)S(1)} %copy-done.1), kind=kLoop, calls=%fused_computation.1 | loop fusion | flops 192 | bytes 1536 | tf_op jit(solution)/shard_map/mul | solution.py:412
  23.9 0.1 copy-done
  24.0 1.6 %broadcast_multiply_fusion = f32[128,128]{1,0:T(8,128)} fusion(f32[128,128]{1,0:T(8,128)} %get-tuple-element.5, f32[128]{0:T(128)S(1)} %copy-done), kind=kLoop, calls=%fused_computation | loop fusion | flops 16384 | bytes 131584 | tf_op jit(solution)/shard_map/mul | solution.py:412
Async XLA Ops:
  22.6 0.7 %copy-start.1 = (f32[2,96]{1,0:T(2,128)S(1)}, f32[2,96]{1,0:T(2,128)}, u32[]{:S(2)}) copy-start(f32[2,96]{1,0:T(2,128)} %get-tuple-element.4) | copy-start | bytes 2308
  23.3 0.7 %copy-start = (f32[128]{0:T(128)S(1)}, f32[128]{0:T(128)}, u32[]{:S(2)}) copy-start(f32[128]{0:T(128)} %param.7) | copy-start | bytes 1540

commit v3 on v2

--- a/solution.py
+++ b/solution.py
@@ -305,6 +305,24 @@
         stats[t, 2 * j + i, 0:1, :] = top
         stats[t, 2 * j + i, 1:2, :] = jnp.sum(terms, axis=0, keepdims=True)
 
+    def tall_tile(t, column_at, column_k, row_at, row_k):
+        wide = nn_dot(set_of(row_at + part, row_k), scaled)
+        projected = (
+            wide[:, :width] + (wide[:, width : 2 * width] + wide[:, 2 * width :])
+        ).astype(jnp.bfloat16)
+        columns = [set_of(column_at + j * part, column_k) for j in range(2)]
+        scores = nt_dot(jnp.concatenate(columns, axis=0), projected)
+        column_bias = bias[t].reshape(total, width)
+        scores = scores + jnp.concatenate([column_bias] * (half // width), axis=1)
+        top = jnp.max(scores, axis=0, keepdims=True)
+        terms = jnp.exp(scores - top)
+        rounded = terms.astype(jnp.bfloat16)
+        sums = (jnp.sum(terms, axis=0, keepdims=True), jnp.zeros_like(top))
+        for j in range(2):
+            kernel_rows[t, j, :, half:] = rounded[j * half : (j + 1) * half]
+            stats[t, 2 * j + 1, 0:1, :] = top
+            stats[t, 2 * j + 1, 1:2, :] = sums[j]
+
     own_t = (2 * tm, base, 0, base, 1)
     middle_t = (1, 0, 1, n_dom, 0)
     other_t = (2 * other, far_base, 0, far_base, 1)
@@ -333,8 +351,8 @@
     weights[steps - 1] = last / jnp.sum(last, axis=0, keepdims=True)
 
     for case in (own_t, middle_t, other_t):
-        for j, i in ((0, 1), (1, 0), (1, 1)):
-            tile(*case, j, i)
+        tile(*case, 1, 0)
+        tall_tile(*case)
 
     score = jnp.zeros((width, width), jnp.float32)
     for t in range(steps - 2, -1, -1):
@@ -367,13 +385,31 @@
             predicted = nt_dot(columns, weight)
             residual = (both[:, :width] - predicted * now).astype(jnp.bfloat16)
             score = score + tn_dot(residual, columns)
-    score_ref[...] = score
+    score_ref[...] = score * p_down
     first = pl.multiple_of(group * rows, rows)
     for k in range(2):
         own = weights[2 * tm + k, pl.ds(first, rows), :]
-        smoothed_ref[k : k + 1, :] = own.T[0:1, :]
+        smoothed_ref[k : k + 1, :] = own.T[0:1, :] * total
     for copy in sends:
         copy.wait_send()
+
+
+def hand_over(a_in, b_in, a_out, b_out, a_held, b_held, sems):
+    arriving = [
+        pltpu.make_async_copy(a_in, a_held, sems.at[0]),
+        pltpu.make_async_copy(b_in, b_held, sems.at[1]),
+    ]
+    leaving = [
+        pltpu.make_async_copy(a_held, a_out, sems.at[2]),
+        pltpu.make_async_copy(b_held, b_out, sems.at[3]),
+    ]
+    for copy in arriving:
+        copy.start()
+    for first, then in zip(arriving, leaving):
+        first.wait()
+        then.start()
+    for copy in leaving:
+        copy.wait()
 
 
 def fused(particles, log_weight, trans_weight, precision):
@@ -409,7 +445,21 @@
             collective_id=0, has_side_effects=True, vmem_limit_bytes=64 * 2**20
         ),
     )(particles, log_weight, trans_weight, precision.reshape(1, width))
-    return smoothed * total, score * precision[:, None]
+    return pl.pallas_call(
+        hand_over,
+        out_shape=(
+            jax.ShapeDtypeStruct((steps_here, rows), jnp.float32),
+            jax.ShapeDtypeStruct((width, width), jnp.float32),
+        ),
+        in_specs=[pl.BlockSpec(memory_space=pltpu.HBM)] * 2,
+        out_specs=(pl.BlockSpec(memory_space=pltpu.HBM),) * 2,
+        scratch_shapes=[
+            pltpu.VMEM((steps_here, rows), jnp.float32),
+            pltpu.VMEM((width, width), jnp.float32),
+            pltpu.SemaphoreType.DMA((4,)),
+        ],
+        compiler_params=pltpu.CompilerParams(vmem_limit_bytes=64 * 2**20),
+    )(smoothed, score)
 
 
 def plan(particles, log_weight, trans_weight, precision):

time: 25.8 us -> 23.8 us (0.922)
  other arithmetic: 2.12 us -> 0 us
  Pallas kernels: 22 us -> 23 us
  local copies, waits for them, and re-layouts: 0.77 us -> 0 us
    mul x2 -> x0, other arithmetic: 2.12 us -> none  [fused(): return (smoothed * total, score * precision[:, None])]
    pallas_call x0 -> x1, Pallas kernels: none -> 1.51 us  [fused(): pl.pallas_call(hand_over, out_shape=(jax.ShapeDtypeStruct((steps_here, ro...]
    unnamed x4 -> x0, local copies, waits for them, and re-layouts: 0.77 us -> none
    pallas_call x1, Pallas kernels: 22 us -> 21.4 us  [fused(): pl.pallas_call(functools.partial(smoother_kernel, n_dom), out_shape=(jax....]
where the time goes in v3:
time: 23.8 us; the launch traced here: 23.6 us
  Pallas kernels  23 us (97%)
  between operations  0.64 us (3%)
    pallas_call x1, Pallas kernels, fused(): pl.pallas_call(functools.partial(smoother_kernel, n_dom), out_shape=(jax....  21.4 us
    pallas_call x1, Pallas kernels, fused(): pl.pallas_call(hand_over, out_shape=(jax.ShapeDtypeStruct((steps_here, ro...  1.51 us

profile of v3, /device:TPU:1, one launch (start us, length us, event | category | flops | bytes accessed | tf_op | source)
XLA Modules:
  0.0 23.6 jit_solution(7625830880356316331)
XLA Ops:
  0.6 21.4 %shard_map.59 = (f32[2,96]{1,0:T(2,128)}, f32[128,128]{1,0:T(8,128)}) custom-call(bf16[2,96,128]{2,1,0:T(8,128)(2,1)} %x_hbm.1, f32[2,96]{1,0:T(2,128)} %lw_hbm.1, bf16[128,128]{1,0:T(8,128)(2,1)} %w_hbm.1, f32[1,128]{1,0:T(1,128)} %bitcast.1), custom_call_target="tpu_custom_call" | custom-call | tf_op jit(solution)/shard_map/pallas_call | solution.py:421
  22.1 1.5 %shard_map.60 = (f32[2,96]{1,0:T(2,128)}, f32[128,128]{1,0:T(8,128)}) custom-call(f32[2,96]{1,0:T(2,128)} %get-tuple-element.4.a_in, f32[128,128]{1,0:T(8,128)} %get-tuple-element.5.b_in), custom_call_target="tpu_custom_call" | custom-call | tf_op jit(solution)/shard_map/pallas_call | solution.py:448

commit v4 on v3

--- a/solution.py
+++ b/solution.py
@@ -317,11 +317,9 @@
         top = jnp.max(scores, axis=0, keepdims=True)
         terms = jnp.exp(scores - top)
         rounded = terms.astype(jnp.bfloat16)
-        sums = (jnp.sum(terms, axis=0, keepdims=True), jnp.zeros_like(top))
+        stats[t, 1, 1:2, :] = jnp.sum(terms, axis=0, keepdims=True)
         for j in range(2):
             kernel_rows[t, j, :, half:] = rounded[j * half : (j + 1) * half]
-            stats[t, 2 * j + 1, 0:1, :] = top
-            stats[t, 2 * j + 1, 1:2, :] = sums[j]
 
     own_t = (2 * tm, base, 0, base, 1)
     middle_t = (1, 0, 1, n_dom, 0)
@@ -356,28 +354,33 @@
 
     score = jnp.zeros((width, width), jnp.float32)
     for t in range(steps - 2, -1, -1):
-        for i in range(2):
-            tops = [stats[t, 2 * j + i, 0:1, :] for j in range(2)]
-            top = jnp.maximum(tops[0], tops[1])
-            scales = [jnp.exp(tops[j] - top) for j in range(2)]
-            norm = sum(scales[j] * stats[t, 2 * j + i, 1:2, :] for j in range(2))
-            for j in range(2):
-                inverse = scales[j] / norm
-                for b in range(half // width):
-                    at = i * half + b * width
-                    inverse_norm[t, j, at : at + width, :] = jnp.broadcast_to(
-                        inverse[:, b * width : (b + 1) * width], (width, width)
-                    ).T
+        tops = [stats[t, 2 * j, 0:1, :] for j in range(2)]
+        top = jnp.maximum(tops[0], tops[1])
+        scales = [jnp.exp(tops[j] - top) for j in range(2)]
+        norm = sum(scales[j] * stats[t, 2 * j, 1:2, :] for j in range(2))
+        inverses = [(0, 0, scales[0] / norm), (1, 0, scales[1] / norm)]
+        inverses.append((0, half, 1.0 / stats[t, 1, 1:2, :]))
+        for j, start, inverse in inverses:
+            for b in range(half // width):
+                at = start + b * width
+                inverse_norm[t, j, at : at + width, :] = jnp.broadcast_to(
+                    inverse[:, b * width : (b + 1) * width], (width, width)
+                ).T
     for t in range(steps - 2, -1, -1):
         at, k = (t // 2) * n_dom, t % 2
         later_at, later_k = ((t + 1) // 2) * n_dom, (t + 1) % 2
-        later = jnp.concatenate([set_of(later_at + i * part, later_k) for i in range(2)], axis=0)
-        later = later.astype(jnp.float32)
+        later = [set_of(later_at + i * part, later_k).astype(jnp.float32) for i in range(2)]
+
+        def weighted(i, j):
+            span = slice(i * half, (i + 1) * half)
+            ratio = weights[t + 1, span, :] * inverse_norm[t, j, span, :]
+            return jnp.concatenate(
+                [(ratio * later[i]).astype(jnp.bfloat16), ratio.astype(jnp.bfloat16)], axis=1
+            )
+
+        far_right = weighted(1, 0)
         for j in range(2):
-            ratio = weights[t + 1] * inverse_norm[t, j]
-            right = jnp.concatenate(
-                [(ratio * later).astype(jnp.bfloat16), ratio.astype(jnp.bfloat16)], axis=1
-            )
+            right = jnp.concatenate([weighted(0, j), far_right], axis=0)
             both = nn_dot(kernel_rows[t, j], right)
             now = both[:, width:]
             weights[t, j * half : (j + 1) * half, :] = now

time: 23.8 us -> 23.9 us (level)
  no operation moved by 1% of the time
where the time goes in v4:
time: 23.9 us; the launch traced here: 23.6 us
  Pallas kernels  23 us (96%)
  between operations  0.64 us (3%)
    pallas_call x1, Pallas kernels, fused(): pl.pallas_call(functools.partial(smoother_kernel, n_dom), out_shape=(jax....  21.5 us
    pallas_call x1, Pallas kernels, fused(): pl.pallas_call(hand_over, out_shape=(jax.ShapeDtypeStruct((steps_here, ro...  1.51 us

profile of v4, /device:TPU:1, one launch (start us, length us, event | category | flops | bytes accessed | tf_op | source)
XLA Modules:
  0.0 23.6 jit_solution(9243590098171681138)
XLA Ops:
  0.6 21.5 %shard_map.59 = (f32[2,96]{1,0:T(2,128)}, f32[128,128]{1,0:T(8,128)}) custom-call(bf16[2,96,128]{2,1,0:T(8,128)(2,1)} %x_hbm.1, f32[2,96]{1,0:T(2,128)} %lw_hbm.1, bf16[128,128]{1,0:T(8,128)(2,1)} %w_hbm.1, f32[1,128]{1,0:T(1,128)} %bitcast.1), custom_call_target="tpu_custom_call" | custom-call | tf_op jit(solution)/shard_map/pallas_call | solution.py:424
  22.1 1.5 %shard_map.60 = (f32[2,96]{1,0:T(2,128)}, f32[128,128]{1,0:T(8,128)}) custom-call(f32[2,96]{1,0:T(2,128)} %get-tuple-element.4.a_in, f32[128,128]{1,0:T(8,128)} %get-tuple-element.5.b_in), custom_call_target="tpu_custom_call" | custom-call | tf_op jit(solution)/shard_map/pallas_call | solution.py:451
